TPU v7x, 32 devices: a whole 2x2x4 slice. The times are simulated.
32 devices in a mesh: seq: 16 (over z, x, core), head: 2 (over y).
Axes of the slice: x: 2, y: 2, z: 4, core: 2. Of those that a mesh axis runs over, the one named last changes fastest.
Arguments:
- features: bfloat16 [8, 32, 8, 512], P(None, 'seq', 'head'), may hold values from -540 to 540
- gn_gain: float32 [512], replicated, may hold values from 0.5 to 1.5
- gn_bias: float32 [512], replicated, may hold values from -3 to 3
- conv_weight: bfloat16 [3, 3, 3, 16, 512], replicated, may hold values from -0.0546875 to 0.0546875
- conv_bias: float32 [16], replicated, may hold values from -3 to 3
- patch_weight: bfloat16 [64, 3072], replicated, may hold values from -0.75 to 0.75
- patch_bias: float32 [3072], replicated, may hold values from -3 to 3
- image_mod: float32 [3, 3072], replicated, may hold values from -3 to 3
- w_qkv: bfloat16 [3072, 3, 2048], P('seq', None, 'head'), may hold values from -5 to 5
- text_ids: int32 [512], replicated, may hold values from 0 to 16383
- text_length: int32 [1], replicated, may hold values from 256 to 512
- text_table: bfloat16 [3072, 16384], P('seq'), may hold values from -60 to 60
- text_mod: float32 [2, 3072], P(None, 'seq'), may hold values from -3 to 3
- w_text: bfloat16 [3072, 2, 2048], P('seq', None, 'head'), may hold values from -2 to 2
- w_out: bfloat16 [2048, 3072], P('head'), may hold values from -0.625 to 0.625
- out_bias: float32 [3072], replicated, may hold values from -3 to 3
Outputs:
- block_out: bfloat16 [8, 16, 4, 3072], P(None, 'seq', 'head')
All inputs are finite; a program needn't handle non-finite values.
Results may differ from a plain program's by a relative error of at most 0.0089.
Values may be sent and summed in bfloat16 or wider, within the bound.
A program may use at most 128 MiB of HBM per device.

v0:
```python
import jax
import jax.numpy as jnp
from jax import lax
from jax.sharding import PartitionSpec as P

HD = 128
GN_GROUPS = 32
CHUNK = 512
eps_norm = 1e-06


def group_gather(piece, group, dim):
    if group == 1:
        return piece
    count = lax.axis_size("seq")
    if group == 2:
        other = lax.ppermute(piece, "seq", [(i, i ^ 1) for i in range(count)])
        first = lax.axis_index("seq") % 2 == 0
        return jnp.concatenate(
            [jnp.where(first, piece, other), jnp.where(first, other, piece)], axis=dim
        )
    members = [list(range(i, i + group)) for i in range(0, count, group)]
    return lax.all_gather(piece, "seq", axis=dim, tiled=True, axis_index_groups=members)


def group_norm(features, gn_gain, gn_bias):
    frame_count, row_count, col_count, chan_count = features.shape
    per_group = chan_count // GN_GROUPS
    values = features.astype(jnp.float32)
    chan_sums = jnp.stack(
        [jnp.sum(values, axis=(0, 1, 2)), jnp.sum(values * values, axis=(0, 1, 2))]
    )
    sums = jnp.sum(chan_sums.reshape(2, GN_GROUPS, per_group), axis=2)
    sums = lax.psum(sums, ("seq", "head"))
    cell_count = (
        frame_count
        * row_count
        * col_count
        * per_group
        * lax.axis_size("seq")
        * lax.axis_size("head")
    )
    mean = sums[0] / cell_count
    scale = lax.rsqrt(sums[1] / cell_count - mean * mean + eps_norm)
    mean = jnp.repeat(mean, per_group)
    scale = jnp.repeat(scale, per_group)
    normed = (values - mean) * scale
    return jax.nn.silu(normed * gn_gain + gn_bias).astype(jnp.bfloat16)


def join_rims(parts, block_dim, dim, unit):
    size = parts.shape[dim]
    blocks = parts.shape[block_dim]
    core = lax.slice_in_dim(parts, unit, size - unit, axis=dim)
    low = lax.slice_in_dim(parts, 0, unit, axis=dim)
    high = lax.slice_in_dim(parts, size - unit, size, axis=dim)
    low = lax.slice_in_dim(low, 1, blocks, axis=block_dim)
    high = lax.slice_in_dim(high, 0, blocks - 1, axis=block_dim)
    pad_low = [(0, 0)] * parts.ndim
    pad_low[block_dim] = (0, 1)
    pad_low[dim] = (size - 3 * unit, 0)
    pad_high = [(0, 0)] * parts.ndim
    pad_high[block_dim] = (1, 0)
    pad_high[dim] = (0, size - 3 * unit)
    return core + jnp.pad(low, pad_low) + jnp.pad(high, pad_high)


def all_patches(activated, conv_weight, conv_bias):
    seq_n, head_n = (lax.axis_size("seq"), lax.axis_size("head"))
    frame_count, row_count, col_count, _ = activated.shape
    chans = conv_weight.shape[3]
    padded = jnp.concatenate([activated[:1], activated[:1], activated], axis=0)
    shares = lax.conv_general_dilated(
        padded[None],
        conv_weight,
        (1, 1, 1),
        ((0, 0), (2, 2), (2, 2)),
        dimension_numbers=("NDHWC", "DHWOI", "NDHWC"),
        preferred_element_type=jnp.float32,
    )[0]
    flat = shares.reshape(-1, 128)
    parts = lax.all_gather(flat, ("seq", "head"), axis=0, tiled=False)
    parts = parts.reshape(seq_n, head_n, frame_count, row_count + 2, (col_count + 2) * chans)
    parts = join_rims(join_rims(parts, 0, 3, 1), 1, 4, chans)
    latent = (parts + jnp.tile(conv_bias, col_count)).astype(jnp.bfloat16)
    blocks = latent.reshape(
        seq_n, head_n, frame_count, row_count // 2, 2, col_count // 2, 2 * chans
    )
    blocks = blocks.transpose(0, 1, 2, 3, 5, 4, 6)
    own = frame_count * (row_count // 2) * (col_count // 2)
    return blocks.reshape(seq_n * head_n * own, 4 * chans)


def modulate(patches, patch_weight, patch_bias, image_mod):
    hidden = jnp.dot(patches, patch_weight, preferred_element_type=jnp.float32) + patch_bias
    center = jnp.mean(hidden, axis=1, keepdims=True)
    offset = hidden - center
    spread = jnp.mean(offset * offset, axis=1, keepdims=True)
    normed = offset * lax.rsqrt(spread + eps_norm)
    return (normed * (1.0 + image_mod[1]) + image_mod[0]).astype(jnp.bfloat16)


def body(
    features,
    gn_gain,
    gn_bias,
    conv_weight,
    conv_bias,
    patch_weight,
    patch_bias,
    image_mod,
    w_qkv,
    text_ids,
    text_length,
    text_table,
    text_mod,
    w_text,
    w_out,
    out_bias,
):
    frame_count, row_count, col_count, _ = features.shape
    width_full = patch_weight.shape[1]
    seq_n, head_n = (lax.axis_size("seq"), lax.axis_size("head"))
    seq_i, head_i = (lax.axis_index("seq"), lax.axis_index("head"))
    depth, _, head_width = w_qkv.shape
    heads_here = head_width // HD
    group = seq_n // heads_here
    cols = head_width // seq_n
    text_count = text_ids.shape[0]
    both = jnp.concatenate([w_qkv, w_text], axis=1).reshape(depth, 5, seq_n, cols)
    both = both.transpose(2, 0, 1, 3).reshape(seq_n, depth, 5 * cols)
    both = lax.all_to_all(both, "seq", split_axis=0, concat_axis=0, tiled=True)
    both = both.reshape(seq_n * depth, 5, cols)
    both = group_gather(both, group, 2)
    w_query, w_image, w_text_full = (both[:, 0], both[:, 1:3], both[:, 3:5])
    chosen = (
        lax.broadcasted_iota(jnp.int32, (text_table.shape[1], text_count), 0) == text_ids[None, :]
    ).astype(jnp.bfloat16)
    own_context = jnp.dot(text_table, chosen, preferred_element_type=jnp.float32).astype(
        jnp.bfloat16
    )
    context = lax.all_gather(own_context, "seq", axis=0, tiled=True).astype(jnp.float32)
    mod = lax.all_gather(text_mod, "seq", axis=1, tiled=True)
    text_mean = jnp.sum(context, axis=0) / width_full
    text_square = jnp.sum(context * context, axis=0) / width_full
    text_scale = lax.rsqrt(text_square - text_mean * text_mean + eps_norm)
    text_normed = (context - text_mean) * text_scale * (1.0 + mod[1][:, None]) + mod[0][:, None]
    text_high = text_normed.astype(jnp.bfloat16)
    text_low = (text_normed - text_high.astype(jnp.float32)).astype(jnp.bfloat16)
    w_text_flat = w_text_full.reshape(width_full, 2 * HD)
    text_kv = sum(
        (
            lax.dot_general(
                part, w_text_flat, (((0,), (0,)), ((), ())), preferred_element_type=jnp.float32
            )
            for part in (text_high, text_low)
        )
    ).astype(jnp.bfloat16)
    activated = group_norm(features, gn_gain, gn_bias)
    patches = all_patches(activated, conv_weight, conv_bias)
    own = patches.shape[0] // (seq_n * head_n)
    part_rows = head_n * own // group
    my_part = seq_i % group
    chunk = min(CHUNK, patches.shape[0])

    def project(rows):
        modulated = modulate(rows, patch_weight, patch_bias, image_mod)
        kv = jnp.dot(
            modulated, w_image.reshape(width_full, 2 * HD), preferred_element_type=jnp.float32
        )
        query = jnp.dot(modulated, w_query, preferred_element_type=jnp.float32)
        query = lax.dynamic_index_in_dim(
            query.reshape(-1, group, part_rows, HD), my_part, axis=1, keepdims=False
        )
        return (kv.astype(jnp.bfloat16), query.reshape(-1, HD).astype(jnp.bfloat16))

    if chunk == patches.shape[0]:
        image_kv, query = project(patches)
    else:
        image_kv, query = lax.map(project, patches.reshape(-1, chunk, patches.shape[1]))
        image_kv = image_kv.reshape(-1, 2 * HD)
        query = query.reshape(-1, HD)
    keys = jnp.concatenate([image_kv[:, :HD], text_kv[:, :HD]], axis=0)
    vals = jnp.concatenate([image_kv[:, HD:], text_kv[:, HD:]], axis=0)
    key_valid = jnp.arange(keys.shape[0], dtype=jnp.int32) < image_kv.shape[0] + text_length[0]
    scores = (
        lax.dot_general(query, keys, (((1,), (1,)), ((), ())), preferred_element_type=jnp.float32)
        / HD
    )
    scores = jnp.where(key_valid[None, :], scores, -1e30)
    probs = jnp.exp(scores - jnp.max(scores, axis=1, keepdims=True))
    totals = jnp.sum(probs, axis=1, keepdims=True)
    attended = (
        jnp.dot(probs.astype(jnp.bfloat16), vals, preferred_element_type=jnp.float32) / totals
    ).astype(jnp.bfloat16)
    attended = attended.reshape(seq_n, part_rows, HD)
    attended = lax.all_to_all(attended, "seq", split_axis=0, concat_axis=0, tiled=True)
    attended = attended.reshape(heads_here, group, part_rows, HD).transpose(1, 2, 0, 3)
    attended = attended.reshape(head_n * own, head_width)
    if head_n == 2:
        halves = attended.reshape(2, own, head_width)
        away = jnp.dot(
            lax.dynamic_index_in_dim(halves, 1 - head_i, 0, keepdims=False),
            w_out,
            preferred_element_type=jnp.float32,
        )
        here = jnp.dot(
            lax.dynamic_index_in_dim(halves, head_i, 0, keepdims=False),
            w_out,
            preferred_element_type=jnp.float32,
        )
        projected = here + lax.ppermute(away, "head", [(0, 1), (1, 0)]) + out_bias
    else:
        projected = (
            lax.psum_scatter(
                jnp.dot(attended, w_out, preferred_element_type=jnp.float32),
                "head",
                scatter_dimension=0,
                tiled=True,
            )
            + out_bias
        )
    own_patches = lax.dynamic_slice_in_dim(patches, (seq_i * head_n + head_i) * own, own, axis=0)
    hidden = jnp.dot(own_patches, patch_weight, preferred_element_type=jnp.float32) + patch_bias
    block_out = (hidden + image_mod[2] * projected).astype(jnp.bfloat16)
    return block_out.reshape(frame_count, row_count // 2, col_count // 2, width_full)


def solution(mesh):
    return jax.shard_map(
        body,
        mesh=mesh,
        in_specs=(
            P(None, "seq", "head", None),
            P(),
            P(),
            P(),
            P(),
            P(),
            P(),
            P(),
            P("seq", None, "head"),
            P(),
            P(),
            P("seq", None),
            P(None, "seq"),
            P("seq", None, "head"),
            P("head", None),
            P(),
        ),
        out_specs=P(None, "seq", "head", None),
        check_vma=False,
    )
```

profile of v0, /device:TPU:0, one launch (start us, length us, event | category | flops | bytes accessed | tf_op | source)
XLA Modules:
  0.0 296.0 jit_solution(9451545067675089896)
XLA Ops:
  11.3 2.6 copy.85
  13.9 7.4 %all-to-all-start = ((bf16[16,192,320]{2,1,0:T(8,128)(2,1)}), bf16[16,192,320]{2,1,0:T(8,128)(2,1)}, u32[]{:S(2)}, u32[]{:S(2)}) async-start(bf16[16,192,320]{2,1,0:T(8,128)(2,1)} %copy.85), calls=%async_computation | async-start | bytes 4718592 | tf_op jit(solution)/shard_map/all_to_all | solution.py:132
  21.5 9.1 %fusion.23 = bf16[192,512]{1,0:T(8,128)(2,1)} fusion(bf16[192,16384]{1,0:T(8,128)(2,1)} %param.27, s32[512]{0:T(512)S(1)} %copy-done.19), kind=kOutput, calls=%fused_computation.34 | convolution fusion | flops 3229712384 | bytes 6490112 | tf_op jit(solution)/shard_map/dot_general | solution.py:139
  31.0 83.9 %psum.7 = f32[2,32]{1,0:T(2,128)S(1)} all-reduce(f32[2,32]{1,0:T(2,128)S(1)} %maximum_reduce_fusion), channel_id=1, replica_groups=mesh['seq'=16,'head'=2] {'seq','head'}, use_global_device_ids=true, to_apply=%region_3.4 | all-reduce | flops 64 | bytes 512 | tf_op jit(solution)/shard_map/psum | solution.py:34
  115.4 4.2 %convolution_reduce_fusion = f32[8,4,6,16]{3,2,1,0:T(8,128)S(1)} fusion(bf16[3,3,3,16,512]{4,3,2,1,0:T(8,128)(2,1)S(1)} %copy-done, bf16[1,10,2,4,512]{4,3,2,1,0:T(4,128)(2,1)S(1)} %maximum_bitcast_fusion.2), kind=kOutput, calls=%fused_computation.36 | convolution fusion | flops 28311552 | bytes 536576 | tf_op jit(solution)/shard_map/conv_general_dilated | solution.py:73
  119.7 68.1 %all_gather.9 = f32[32,24,128]{2,1,0:T(8,128)S(1)} all-gather(f32[1,24,128]{2,1,0:T(8,128)S(1)} %all_gather_reshape_squeeze.3), channel_id=1, replica_groups=mesh['seq'=16,'head'=2] {'seq','head'}, dimensions={0}, use_global_device_ids=true | all-gather | bytes 405504 | tf_op jit(solution)/shard_map/all_gather | solution.py:82
  189.6 3.6 %add_reduce_fusion = (f32[512]{0:T(512)S(1)}, f32[512,3072]{1,0:T(8,128)}) fusion(f32[3072]{0:T(1024)S(1)} %copy-done.11, bf16[512,64]{1,0:T(8,128)(2,1)S(1)} %reshape.100, bf16[64,3072]{1,0:T(8,128)(2,1)S(1)} %copy-done.7), kind=kOutput, calls=%fused_computation.15 | convolution fusion | flops 204471808 | bytes 6764544 | tf_op jit(solution)/shard_map/dot_general | solution.py:95
  193.2 17.4 %all-gather = f32[16,192,2]{1,2,0:T(2,128)S(1)} all-gather(f32[1,192,2]{1,2,0:T(2,128)S(1)} %bitcast.101), channel_id=1, replica_groups=mesh['seq'=16,'head'=2] {'seq'}, dimensions={0}, use_global_device_ids=true | all-gather | bytes 26112 | tf_op jit(solution)/shard_map/all_gather | solution.py:143
  210.8 3.9 %copy.86 = bf16[16,192,320]{1,0,2:T(8,128)(2,1)S(1)} copy(bf16[16,192,320]{2,1,0:T(8,128)(2,1)} %all-to-all-done) | data formatting | bytes 3932160 | tf_op jit(solution)/shard_map/all_to_all | solution.py:132
  214.7 3.7 %reshape.103 = bf16[3072,5,64]{0,2,1:T(8,128)(2,1)} reshape(bf16[16,192,320]{1,0,2:T(8,128)(2,1)S(1)} %copy.86) | data formatting | bytes 3932160 | tf_op jit(solution)/shard_map/reshape | solution.py:133
  218.7 3.7 %multiply_reduce_fusion = f32[512]{0:T(512)S(1)} fusion(f32[512,3072]{1,0:T(8,128)} %get-tuple-element.29, f32[512]{0:T(512)S(1)} %broadcast_multiply_fusion.1, f32[3072]{0:T(1024)S(1)} %copy-done.11), kind=kLoop, calls=%fused_computation.14 | loop fusion | flops 6290944 | bytes 6307840 | tf_op jit(solution)/shard_map/reduce_sum | solution.py:98
  223.2 6.3 %add_convert_fusion = bf16[512,3072]{1,0:T(8,128)(2,1)} fusion(f32[512,3072]{1,0:T(8,128)} %get-tuple-element.29, f32[3072]{0:T(1024)S(1)} %bitcast.95, f32[3072]{0:T(1024)S(1)} %bitcast.96, f32[512]{0:T(512)S(1)} %add_rsqrt_fusion.1, f32[512]{0:T(512)S(1)} %broadcast_multiply_fusion.1, f32[3072]{0:T(1024)S(1)} %copy-done.11), kind=kLoop, calls=%fused_computation.13 | loop fusion | flops 9437184 | bytes 9478144 | tf_op jit(solution)/shard_map/convert_element_type | solution.py:100
  229.5 3.1 %copy.87 = bf16[3072,5,64]{2,0,1:T(8,128)(2,1)} copy(bf16[3072,5,64]{0,2,1:T(8,128)(2,1)S(1)} %copy-done.5) | data formatting | bytes 3932160 | tf_op jit(solution)/shard_map/reshape | solution.py:133
  232.6 4.7 %copy.88 = bf16[3072,5,64]{2,0,1:T(8,128)(2,1)} copy(bf16[3072,5,64]{0,2,1:T(8,128)(2,1)} %collective-permute-done) | data formatting | bytes 3932160 | tf_op jit(solution)/shard_map/ppermute | solution.py:17
  237.3 3.6 %broadcast_select_fusion.1 = (bf16[3072,5,64]{2,0,1:T(8,128)(2,1)S(1)}, bf16[3072,5,64]{2,0,1:T(8,128)(2,1)S(1)}) fusion(bf16[3072,5,64]{2,0,1:T(8,128)(2,1)} %copy.87, bf16[3072,5,64]{2,0,1:T(8,128)(2,1)} %copy.88, pred[]{:T(512)S(6)} %eq.14), kind=kLoop, calls=%fused_computation.17 | loop fusion | flops 1966080 | bytes 7864321 | tf_op jit(solution)/shard_map/jit(_where)/select_n | solution.py:20
  240.9 3.3 %pad_maximum_fusion.2 = (bf16[3072,2,128]{2,0,1:T(8,128)(2,1)S(1)}, bf16[3072,2,128]{2,0,1:T(8,128)(2,1)}) fusion(bf16[3072,5,64]{2,0,1:T(8,128)(2,1)S(1)} %get-tuple-element.12, bf16[3072,5,64]{2,0,1:T(8,128)(2,1)S(1)} %get-tuple-element.11), kind=kLoop, calls=%fused_computation.27 | loop fusion | flops 6291456 | bytes 7077888 | tf_op jit(solution)/shard_map/slice | solution.py:135
  248.6 3.5 %fusion.27 = bf16[16,2,16,128]{3,2,1,0:T(8,128)(2,1)S(1)} fusion(bf16[16,2,16,3072]{3,2,1,0:T(8,128)(2,1)} %bitcast.80, bf16[3072,5,64]{2,0,1:T(8,128)(2,1)} %copy-done.3, bf16[3072,5,64]{2,0,1:T(8,128)(2,1)} %copy-done.2), kind=kOutput, calls=%fused_computation.42 | convolution fusion | flops 404226048 | bytes 7208960 | tf_op jit(solution)/shard_map/dot_general | solution.py:171
  253.5 2.8 convert_reduce_fusion
  256.2 4.0 %fusion.43 = f32[512,256]{1,0:T(8,128)S(1)} fusion(bf16[3072,256]{0,1:T(8,128)(2,1)S(1)} %bitcast.83, bf16[3072,512]{1,0:T(8,128)(2,1)} %all-gather.3.cloned.1.call-done, f32[3072]{0:T(1024)S(1)} %bitcast.99, f32[3072]{0:T(1024)S(1)} %bitcast.97, f32[512]{0:T(512)S(1)} %get-tuple-element.27, f32[512]{0:T(512)S(1)} %get-tuple-element.26), kind=kOutput, calls=%fused_computation.58 | convolution fusion | flops 814743552 | bytes 5271552 | tf_op jit(solution)/shard_map/dot_general | solution.py:153
  264.1 3.6 %all-to-all-start.1 = ((bf16[16,16,128]{2,1,0:T(8,128)(2,1)}), bf16[16,16,128]{2,1,0:T(8,128)(2,1)S(1)}, u32[]{:S(2)}, u32[]{:S(2)}) async-start(bf16[16,16,128]{2,1,0:T(8,128)(2,1)} %bitcast.24), calls=%async_computation.1 | async-start | bytes 131072 | tf_op jit(solution)/shard_map/all_to_all | solution.py:197
  267.7 6.8 %all-to-all-done.1 = bf16[16,16,128]{2,1,0:T(8,128)(2,1)S(1)} async-done(((bf16[16,16,128]{2,1,0:T(8,128)(2,1)}), bf16[16,16,128]{2,1,0:T(8,128)(2,1)S(1)}, u32[]{:S(2)}, u32[]{:S(2)}) %all-to-all-start.1) | async-done | bytes 65568 | tf_op jit(solution)/shard_map/all_to_all | solution.py:197
  274.6 3.8 %fusion.51 = f32[16,3072]{1,0:T(8,128)S(1)} fusion(bf16[1024,3072]{1,0:T(8,128)(2,1)} %param.30, bf16[2,16,1024]{2,1,0:T(8,128)(2,1)S(1)} %bitcast.89, s32[]{:T(128)S(6)} %select_n.47), kind=kOutput, calls=%fused_computation.73 | convolution fusion | flops 100663296 | bytes 6520836 | tf_op jit(solution)/shard_map/dot_general | solution.py:202
  279.2 5.5 %collective-permute-done.1 = f32[16,3072]{1,0:T(8,128)S(1)} collective-permute-done((f32[16,3072]{1,0:T(8,128)S(1)}, f32[16,3072]{1,0:T(8,128)S(1)}, u32[]{:S(2)}, u32[]{:S(2)}) %collective-permute-start.1) | collective-permute-done | bytes 196640 | tf_op jit(solution)/shard_map/ppermute | solution.py:212
  284.8 3.7 %fusion.12 = bf16[16,3072]{1,0:T(8,128)(2,1)S(1)} fusion(f32[16,3072]{1,0:T(8,128)S(1)} %convolution_add_fusion, f32[16,3072]{1,0:T(8,128)S(1)} %collective-permute-done.1, bf16[1024,3072]{1,0:T(8,128)(2,1)} %param.30, f32[3072]{0:T(1024)S(1)} %copy-done.14, f32[3072]{0:T(1024)S(1)} %bitcast.94, bf16[2,16,1024]{2,1,0:T(8,128)(2,1)S(1)} %bitcast.90, ...), kind=kOutput, calls=%fused_computation.23 | convolution fusion | flops 100909056 | bytes 6840324 | tf_op jit(solution)/shard_map/dot_general | solution.py:207
  (97 shorter events, 18.9 us)
Async XLA Ops:
  6.5 108.8 %copy-start = (bf16[3,3,3,16,512]{4,3,2,1,0:T(8,128)(2,1)S(1)}, bf16[3,3,3,16,512]{4,3,2,1,0:T(8,128)(2,1)}, u32[]{:S(2)}) copy-start(bf16[3,3,3,16,512]{4,3,2,1,0:T(8,128)(2,1)} %param.19) | copy-start | bytes 1327108
  11.3 10.1 %copy-start.19 = (s32[512]{0:T(512)S(1)}, s32[512]{0:T(512)}, u32[]{:S(2)}) copy-start(s32[512]{0:T(512)} %param.25) | copy-start | bytes 6148
  13.9 196.8 %all-to-all-start = ((bf16[16,192,320]{2,1,0:T(8,128)(2,1)}), bf16[16,192,320]{2,1,0:T(8,128)(2,1)}, u32[]{:S(2)}, u32[]{:S(2)}) async-start(bf16[16,192,320]{2,1,0:T(8,128)(2,1)} %copy.85), calls=%async_computation | async-start | bytes 4718592 | tf_op jit(solution)/shard_map/all_to_all | solution.py:132
  21.4 9.3 %copy-start.12 = (bf16[8,2,4,512]{3,2,1,0:T(4,128)(2,1)S(1)}, bf16[8,2,4,512]{3,2,1,0:T(4,128)(2,1)}, u32[]{:S(2)}) copy-start(bf16[8,2,4,512]{3,2,1,0:T(4,128)(2,1)} %param.16) | copy-start | bytes 196612
  21.4 93.8 %copy-start.15 = (f32[512]{0:T(512)S(1)}, f32[512]{0:T(512)}, u32[]{:S(2)}) copy-start(f32[512]{0:T(512)} %param.18) | copy-start | bytes 6148
  21.4 93.8 %copy-start.16 = (f32[512]{0:T(512)S(1)}, f32[512]{0:T(512)}, u32[]{:S(2)}) copy-start(f32[512]{0:T(512)} %param.17) | copy-start | bytes 6148
  21.4 167.0 %copy-start.18 = (f32[16]{0:T(128)S(1)}, f32[16]{0:T(128)}, u32[]{:S(2)}) copy-start(f32[16]{0:T(128)} %param.20) | copy-start | bytes 196
  21.4 232.0 %all-gather.3.cloned.1.call-start = ((), (), s32[]{:S(2)}) async-start(), calls=%async_computation.2 | async-start | bytes 3342336 | tf_op jit(solution)/shard_map/all_gather | solution.py:142
  30.6 158.9 %copy-start.7 = (bf16[64,3072]{1,0:T(8,128)(2,1)S(1)}, bf16[64,3072]{1,0:T(8,128)(2,1)}, u32[]{:S(2)}) copy-start(bf16[64,3072]{1,0:T(8,128)(2,1)} %param.21) | copy-start | bytes 1179652
  30.6 158.9 %copy-start.11 = (f32[3072]{0:T(1024)S(1)}, f32[3072]{0:T(1024)}, u32[]{:S(2)}) copy-start(f32[3072]{0:T(1024)} %param.22) | copy-start | bytes 36868
  189.5 3.7 %copy-start.10 = (bf16[512,64]{1,0:T(8,128)(2,1)}, bf16[512,64]{1,0:T(8,128)(2,1)S(1)}, u32[]{:S(2)}) copy-start(bf16[512,64]{1,0:T(8,128)(2,1)S(1)} %reshape.100) | copy-start | bytes 196612
  189.6 3.6 %copy-start.17 = (f32[2,192]{1,0:T(2,128)S(1)}, f32[2,192]{1,0:T(2,128)}, u32[]{:S(2)}) copy-start(f32[2,192]{1,0:T(2,128)} %param.28) | copy-start | bytes 4612
  218.4 4.7 %copy-start.13 = (f32[3,3072]{1,0:T(4,128)S(1)}, f32[3,3072]{1,0:T(4,128)}, u32[]{:S(2)}) copy-start(f32[3,3072]{1,0:T(4,128)} %param.23) | copy-start | bytes 110596
  218.4 14.2 %collective-permute-start = (bf16[3072,5,64]{0,2,1:T(8,128)(2,1)}, bf16[3072,5,64]{0,2,1:T(8,128)(2,1)}, u32[]{:S(2)}, u32[]{:S(2)}) collective-permute-start(bf16[3072,5,64]{0,2,1:T(8,128)(2,1)} %reshape.103), channel_id=1, source_target_pairs={{0,2},{2,0},{4,6},{6,4},{8,10},{10,8},{12,14},{14,12},{16,18},{18,... | collective-permute-start | bytes 5898248 | tf_op jit(solution)/shard_map/ppermute | solution.py:17
  223.2 6.3 %copy-start.5 = (bf16[3072,5,64]{0,2,1:T(8,128)(2,1)S(1)}, bf16[3072,5,64]{0,2,1:T(8,128)(2,1)}, u32[]{:S(2)}) copy-start(bf16[3072,5,64]{0,2,1:T(8,128)(2,1)} %reshape.103) | copy-start | bytes 5898244
  240.9 3.5 %copy-start.3 = (bf16[3072,5,64]{2,0,1:T(8,128)(2,1)}, bf16[3072,5,64]{2,0,1:T(8,128)(2,1)S(1)}, u32[]{:S(2)}) copy-start(bf16[3072,5,64]{2,0,1:T(8,128)(2,1)S(1)} %get-tuple-element.12) | copy-start | bytes 5898244
  248.6 3.6 %copy-start.4 = (bf16[512,3072]{1,0:T(8,128)(2,1)S(1)}, bf16[512,3072]{1,0:T(8,128)(2,1)}, u32[]{:S(2)}) copy-start(bf16[512,3072]{1,0:T(8,128)(2,1)} %add_convert_fusion) | copy-start | bytes 9437188
  248.6 3.8 %copy-start.9 = (bf16[3072,2,128]{0,2,1:T(8,128)(2,1)S(1)}, bf16[3072,2,128]{0,2,1:T(8,128)(2,1)}, u32[]{:S(2)}) copy-start(bf16[3072,2,128]{0,2,1:T(8,128)(2,1)} %copy.91) | copy-start | bytes 4718596
  252.4 3.9 %copy-start.8 = (bf16[3072,2,128]{0,2,1:T(8,128)(2,1)S(1)}, bf16[3072,2,128]{0,2,1:T(8,128)(2,1)}, u32[]{:S(2)}) copy-start(bf16[3072,2,128]{0,2,1:T(8,128)(2,1)} %copy.93) | copy-start | bytes 4718596
  256.2 4.0 %copy-start.6 = (bf16[3072,512]{1,0:T(8,128)(2,1)S(1)}, bf16[3072,512]{1,0:T(8,128)(2,1)}, u32[]{:S(2)}) copy-start(bf16[3072,512]{1,0:T(8,128)(2,1)} %all-gather.3.cloned.1.call-done) | copy-start | bytes 9437188
  264.1 20.7 %copy-start.14 = (f32[3072]{0:T(1024)S(1)}, f32[3072]{0:T(1024)}, u32[]{:S(2)}) copy-start(f32[3072]{0:T(1024)} %param.31) | copy-start | bytes 36868
  264.1 10.5 %all-to-all-start.1 = ((bf16[16,16,128]{2,1,0:T(8,128)(2,1)}), bf16[16,16,128]{2,1,0:T(8,128)(2,1)S(1)}, u32[]{:S(2)}, u32[]{:S(2)}) async-start(bf16[16,16,128]{2,1,0:T(8,128)(2,1)} %bitcast.24), calls=%async_computation.1 | async-start | bytes 131072 | tf_op jit(solution)/shard_map/all_to_all | solution.py:197
  274.6 14.6 %copy-start.1 = (bf16[3,3,3,16,512]{4,3,2,1,0:T(8,128)(2,1)S(1)}, bf16[3,3,3,16,512]{4,3,2,1,0:T(8,128)(2,1)}, u32[]{:S(2)}) copy-start(bf16[3,3,3,16,512]{4,3,2,1,0:T(8,128)(2,1)} %param.19) | copy-start | bytes 1327108
  278.4 6.4 %collective-permute-start.1 = (f32[16,3072]{1,0:T(8,128)S(1)}, f32[16,3072]{1,0:T(8,128)S(1)}, u32[]{:S(2)}, u32[]{:S(2)}) collective-permute-start(f32[16,3072]{1,0:T(8,128)S(1)} %fusion.51), channel_id=1, source_target_pairs={{0,1},{1,0},{2,3},{3,2},{4,5},{5,4},{6,7},{7,6},{8,9},{9,8},{10,11... | collective-permute-start | bytes 589832 | tf_op jit(solution)/shard_map/ppermute | solution.py:212
  (1 other events, 3.4 us)
Sparse Core Ops, SparseCore 0:
  30.8 66.3 all-gather.2
where the time goes:
time: 297 us; the launch traced here: 296 us
  blocking collectives  169 us (57%)
  matrix products  37.4 us (13%)
  local copies, waits for them, and re-layouts  29.8 us (10%)
  other arithmetic  21.1 us (7%)
  between operations  14.6 us (5%)
  waiting for transfers between devices  12.4 us (4%)
  starting transfers between devices  11.4 us (4%)
    psum x1, blocking collectives, group_norm(): sums = lax.psum(sums, ('seq', 'head'))  83.9 us
    all_gather x1, blocking collectives, all_patches(): parts = lax.all_gather(flat, ('seq', 'head'), axis=0, tiled=False)  68.1 us
    all_gather x1, blocking collectives, body(): mod = lax.all_gather(text_mod, 'seq', axis=1, tiled=True)  17.4 us
    dot_general x1, matrix products, body(): jnp.dot(text_table, chosen, preferred_element_type=jnp.float32)  9.15 us
    all_to_all x1, starting transfers between devices, body(): both = lax.all_to_all(both, 'seq', split_axis=0, concat_axis=0, tiled=True)  7.4 us
    all_to_all x1, waiting for transfers between devices, body(): lax.all_to_all(attended, 'seq', split_axis=0, concat_axis=0, tiled=True)  6.85 us
    reshape x2, local copies, waits for them, and re-layouts, body(): both = both.reshape(seq_n * depth, 5, cols)  6.84 us
    convert_element_type x1, other arithmetic, modulate(): return (normed * (1.0 + image_mod[1]) + image_mod[0]).astype(jnp.bfloat16)  6.3 us
  transfers between devices with their start and end apart: 5, of which 2 were waited for; matrix products, arithmetic and copies ran while one was open for 21% of the time, Pallas kernels for 0%

commit v1 on v0

--- a/solution.py
+++ b/solution.py
@@ -31,7 +31,8 @@
         [jnp.sum(values, axis=(0, 1, 2)), jnp.sum(values * values, axis=(0, 1, 2))]
     )
     sums = jnp.sum(chan_sums.reshape(2, GN_GROUPS, per_group), axis=2)
-    sums = lax.psum(sums, ("seq", "head"))
+    pieces = lax.all_gather(sums, ("seq", "head"), axis=0, tiled=False)
+    sums = pieces.sum(axis=0)
     cell_count = (
         frame_count
         * row_count

time: 297 us -> 310 us (1.044)
  blocking collectives: 169 us -> 183 us
    all_gather x0 -> x1, blocking collectives: none -> 97.5 us  [group_norm(): pieces = lax.all_gather(sums, ('seq', 'head'), axis=0, tiled=False)]
    psum x1 -> x0, blocking collectives: 83.9 us -> none  [group_norm(): sums = lax.psum(sums, ('seq', 'head'))]
  transfers between devices with their start and end apart: 5 -> 5, of which waited for: 2 -> 2; matrix products, arithmetic and copies ran while one was open for 21% -> 20% of each run, Pallas kernels for 0% -> 0%
where the time goes in v1:
time: 310 us; the launch traced here: 309 us
  blocking collectives  183 us (59%)
  matrix products  37.4 us (12%)
  local copies, waits for them, and re-layouts  29.8 us (10%)
  other arithmetic  21.1 us (7%)
  between operations  14.6 us (5%)
  waiting for transfers between devices  12.4 us (4%)
  starting transfers between devices  11.4 us (4%)
    all_gather x1, blocking collectives, group_norm(): pieces = lax.all_gather(sums, ('seq', 'head'), axis=0, tiled=False)  97.5 us
    all_gather x1, blocking collectives, all_patches(): parts = lax.all_gather(flat, ('seq', 'head'), axis=0, tiled=False)  67.9 us
    all_gather x1, blocking collectives, body(): mod = lax.all_gather(text_mod, 'seq', axis=1, tiled=True)  17.4 us
    dot_general x1, matrix products, body(): jnp.dot(text_table, chosen, preferred_element_type=jnp.float32)  9.15 us
    all_to_all x1, starting transfers between devices, body(): both = lax.all_to_all(both, 'seq', split_axis=0, concat_axis=0, tiled=True)  7.4 us
    all_to_all x1, waiting for transfers between devices, body(): lax.all_to_all(attended, 'seq', split_axis=0, concat_axis=0, tiled=True)  6.85 us
    reshape x2, local copies, waits for them, and re-layouts, body(): both = both.reshape(seq_n * depth, 5, cols)  6.84 us
    convert_element_type x1, other arithmetic, modulate(): return (normed * (1.0 + image_mod[1]) + image_mod[0]).astype(jnp.bfloat16)  6.3 us
  transfers between devices with their start and end apart: 5, of which 2 were waited for; matrix products, arithmetic and copies ran while one was open for 20% of the time, Pallas kernels for 0%

profile of v1, /device:TPU:0, one launch (start us, length us, event | category | flops | bytes accessed | tf_op | source)
XLA Modules:
  0.0 309.5 jit_solution(18129063665708863828)
XLA Ops:
  11.3 2.6 copy.85
  13.9 7.4 %all-to-all-start = ((bf16[16,192,320]{2,1,0:T(8,128)(2,1)}), bf16[16,192,320]{2,1,0:T(8,128)(2,1)}, u32[]{:S(2)}, u32[]{:S(2)}) async-start(bf16[16,192,320]{2,1,0:T(8,128)(2,1)} %copy.85), calls=%async_computation | async-start | bytes 4718592 | tf_op jit(solution)/shard_map/all_to_all | solution.py:133
  21.5 9.1 %fusion.23 = bf16[192,512]{1,0:T(8,128)(2,1)} fusion(bf16[192,16384]{1,0:T(8,128)(2,1)} %param.27, s32[512]{0:T(512)S(1)} %copy-done.19), kind=kOutput, calls=%fused_computation.34 | convolution fusion | flops 3229712384 | bytes 6490112 | tf_op jit(solution)/shard_map/dot_general | solution.py:140
  31.0 97.5 %all-gather.1 = f32[32,2,32]{2,1,0:T(2,128)S(1)} all-gather(f32[1,2,32]{2,1,0:T(2,128)S(1)} %bitcast.102), channel_id=2, replica_groups=mesh['seq'=16,'head'=2] {'seq','head'}, dimensions={0}, use_global_device_ids=true | all-gather | bytes 8448 | tf_op jit(solution)/shard_map/all_gather | solution.py:34
  129.1 4.2 %convolution_reduce_fusion = f32[8,4,6,16]{3,2,1,0:T(8,128)S(1)} fusion(bf16[3,3,3,16,512]{4,3,2,1,0:T(8,128)(2,1)S(1)} %copy-done, bf16[1,10,2,4,512]{4,3,2,1,0:T(4,128)(2,1)S(1)} %maximum_bitcast_fusion.2), kind=kOutput, calls=%fused_computation.36 | convolution fusion | flops 28311552 | bytes 536576 | tf_op jit(solution)/shard_map/conv_general_dilated | solution.py:74
  133.4 67.9 %all_gather.17 = f32[32,24,128]{2,1,0:T(8,128)S(1)} all-gather(f32[1,24,128]{2,1,0:T(8,128)S(1)} %all_gather_reshape_squeeze.3), channel_id=1, replica_groups=mesh['seq'=16,'head'=2] {'seq','head'}, dimensions={0}, use_global_device_ids=true | all-gather | bytes 405504 | tf_op jit(solution)/shard_map/all_gather | solution.py:83
  203.0 3.6 %add_reduce_fusion = (f32[512]{0:T(512)S(1)}, f32[512,3072]{1,0:T(8,128)}) fusion(f32[3072]{0:T(1024)S(1)} %copy-done.11, bf16[512,64]{1,0:T(8,128)(2,1)S(1)} %reshape.100, bf16[64,3072]{1,0:T(8,128)(2,1)S(1)} %copy-done.7), kind=kOutput, calls=%fused_computation.15 | convolution fusion | flops 204471808 | bytes 6764544 | tf_op jit(solution)/shard_map/dot_general | solution.py:96
  206.6 17.4 %all-gather.2 = f32[16,192,2]{1,2,0:T(2,128)S(1)} all-gather(f32[1,192,2]{1,2,0:T(2,128)S(1)} %bitcast.103), channel_id=1, replica_groups=mesh['seq'=16,'head'=2] {'seq'}, dimensions={0}, use_global_device_ids=true | all-gather | bytes 26112 | tf_op jit(solution)/shard_map/all_gather | solution.py:144
  224.2 3.9 %copy.86 = bf16[16,192,320]{1,0,2:T(8,128)(2,1)S(1)} copy(bf16[16,192,320]{2,1,0:T(8,128)(2,1)} %all-to-all-done) | data formatting | bytes 3932160 | tf_op jit(solution)/shard_map/all_to_all | solution.py:133
  228.1 3.7 %reshape.103 = bf16[3072,5,64]{0,2,1:T(8,128)(2,1)} reshape(bf16[16,192,320]{1,0,2:T(8,128)(2,1)S(1)} %copy.86) | data formatting | bytes 3932160 | tf_op jit(solution)/shard_map/reshape | solution.py:134
  232.2 3.7 %multiply_reduce_fusion = f32[512]{0:T(512)S(1)} fusion(f32[512,3072]{1,0:T(8,128)} %get-tuple-element.29, f32[512]{0:T(512)S(1)} %broadcast_multiply_fusion.1, f32[3072]{0:T(1024)S(1)} %copy-done.11), kind=kLoop, calls=%fused_computation.14 | loop fusion | flops 6290944 | bytes 6307840 | tf_op jit(solution)/shard_map/reduce_sum | solution.py:99
  236.6 6.3 %add_convert_fusion = bf16[512,3072]{1,0:T(8,128)(2,1)} fusion(f32[512,3072]{1,0:T(8,128)} %get-tuple-element.29, f32[3072]{0:T(1024)S(1)} %bitcast.96, f32[3072]{0:T(1024)S(1)} %bitcast.97, f32[512]{0:T(512)S(1)} %add_rsqrt_fusion.1, f32[512]{0:T(512)S(1)} %broadcast_multiply_fusion.1, f32[3072]{0:T(1024)S(1)} %copy-done.11), kind=kLoop, calls=%fused_computation.13 | loop fusion | flops 9437184 | bytes 9478144 | tf_op jit(solution)/shard_map/convert_element_type | solution.py:101
  242.9 3.1 copy.87
  246.0 4.7 %copy.88 = bf16[3072,5,64]{2,0,1:T(8,128)(2,1)} copy(bf16[3072,5,64]{0,2,1:T(8,128)(2,1)} %collective-permute-done) | data formatting | bytes 3932160 | tf_op jit(solution)/shard_map/ppermute | solution.py:17
  250.7 3.6 %broadcast_select_fusion.1 = (bf16[3072,5,64]{2,0,1:T(8,128)(2,1)S(1)}, bf16[3072,5,64]{2,0,1:T(8,128)(2,1)S(1)}) fusion(bf16[3072,5,64]{2,0,1:T(8,128)(2,1)} %copy.87, bf16[3072,5,64]{2,0,1:T(8,128)(2,1)} %copy.88, pred[]{:T(512)S(6)} %eq.14), kind=kLoop, calls=%fused_computation.17 | loop fusion | flops 1966080 | bytes 7864321 | tf_op jit(solution)/shard_map/jit(_where)/select_n | solution.py:20
  254.4 3.3 %pad_maximum_fusion.2 = (bf16[3072,2,128]{2,0,1:T(8,128)(2,1)S(1)}, bf16[3072,2,128]{2,0,1:T(8,128)(2,1)}) fusion(bf16[3072,5,64]{2,0,1:T(8,128)(2,1)S(1)} %get-tuple-element.12, bf16[3072,5,64]{2,0,1:T(8,128)(2,1)S(1)} %get-tuple-element.11), kind=kLoop, calls=%fused_computation.27 | loop fusion | flops 6291456 | bytes 7077888 | tf_op jit(solution)/shard_map/slice | solution.py:136
  262.0 3.5 %fusion.27 = bf16[16,2,16,128]{3,2,1,0:T(8,128)(2,1)S(1)} fusion(bf16[16,2,16,3072]{3,2,1,0:T(8,128)(2,1)} %bitcast.81, bf16[3072,5,64]{2,0,1:T(8,128)(2,1)} %copy-done.3, bf16[3072,5,64]{2,0,1:T(8,128)(2,1)} %copy-done.2), kind=kOutput, calls=%fused_computation.42 | convolution fusion | flops 404226048 | bytes 7208960 | tf_op jit(solution)/shard_map/dot_general | solution.py:172
  266.9 2.8 convert_reduce_fusion
  269.7 4.0 %fusion.43 = f32[512,256]{1,0:T(8,128)S(1)} fusion(bf16[3072,256]{0,1:T(8,128)(2,1)S(1)} %bitcast.84, bf16[3072,512]{1,0:T(8,128)(2,1)} %all-gather.5.cloned.1.call-done, f32[3072]{0:T(1024)S(1)} %bitcast.100, f32[3072]{0:T(1024)S(1)} %bitcast.98, f32[512]{0:T(512)S(1)} %get-tuple-element.27, f32[512]{0:T(512)S(1)} %get-tuple-element.26), kind=kOutput, calls=%fused_computation.58 | convolution fusion | flops 814743552 | bytes 5271552 | tf_op jit(solution)/shard_map/dot_general | solution.py:154
  277.5 3.6 %all-to-all-start.1 = ((bf16[16,16,128]{2,1,0:T(8,128)(2,1)}), bf16[16,16,128]{2,1,0:T(8,128)(2,1)S(1)}, u32[]{:S(2)}, u32[]{:S(2)}) async-start(bf16[16,16,128]{2,1,0:T(8,128)(2,1)} %bitcast.25), calls=%async_computation.1 | async-start | bytes 131072 | tf_op jit(solution)/shard_map/all_to_all | solution.py:198
  281.2 6.8 %all-to-all-done.1 = bf16[16,16,128]{2,1,0:T(8,128)(2,1)S(1)} async-done(((bf16[16,16,128]{2,1,0:T(8,128)(2,1)}), bf16[16,16,128]{2,1,0:T(8,128)(2,1)S(1)}, u32[]{:S(2)}, u32[]{:S(2)}) %all-to-all-start.1) | async-done | bytes 65568 | tf_op jit(solution)/shard_map/all_to_all | solution.py:198
  288.0 3.8 %fusion.51 = f32[16,3072]{1,0:T(8,128)S(1)} fusion(bf16[1024,3072]{1,0:T(8,128)(2,1)} %param.30, bf16[2,16,1024]{2,1,0:T(8,128)(2,1)S(1)} %bitcast.90, s32[]{:T(128)S(6)} %select_n.47), kind=kOutput, calls=%fused_computation.73 | convolution fusion | flops 100663296 | bytes 6520836 | tf_op jit(solution)/shard_map/dot_general | solution.py:203
  292.7 5.5 %collective-permute-done.1 = f32[16,3072]{1,0:T(8,128)S(1)} collective-permute-done((f32[16,3072]{1,0:T(8,128)S(1)}, f32[16,3072]{1,0:T(8,128)S(1)}, u32[]{:S(2)}, u32[]{:S(2)}) %collective-permute-start.1) | collective-permute-done | bytes 196640 | tf_op jit(solution)/shard_map/ppermute | solution.py:213
  298.2 3.7 %fusion.12 = bf16[16,3072]{1,0:T(8,128)(2,1)S(1)} fusion(f32[16,3072]{1,0:T(8,128)S(1)} %convolution_add_fusion, f32[16,3072]{1,0:T(8,128)S(1)} %collective-permute-done.1, bf16[1024,3072]{1,0:T(8,128)(2,1)} %param.30, f32[3072]{0:T(1024)S(1)} %copy-done.14, f32[3072]{0:T(1024)S(1)} %bitcast.95, bf16[2,16,1024]{2,1,0:T(8,128)(2,1)S(1)} %bitcast.91, ...), kind=kOutput, calls=%fused_computation.23 | convolution fusion | flops 100909056 | bytes 6840324 | tf_op jit(solution)/shard_map/dot_general | solution.py:208
  (98 shorter events, 18.9 us)
Async XLA Ops:
  6.5 122.5 %copy-start = (bf16[3,3,3,16,512]{4,3,2,1,0:T(8,128)(2,1)S(1)}, bf16[3,3,3,16,512]{4,3,2,1,0:T(8,128)(2,1)}, u32[]{:S(2)}) copy-start(bf16[3,3,3,16,512]{4,3,2,1,0:T(8,128)(2,1)} %param.19) | copy-start | bytes 1327108
  11.3 10.1 %copy-start.19 = (s32[512]{0:T(512)S(1)}, s32[512]{0:T(512)}, u32[]{:S(2)}) copy-start(s32[512]{0:T(512)} %param.25) | copy-start | bytes 6148
  13.9 210.2 %all-to-all-start = ((bf16[16,192,320]{2,1,0:T(8,128)(2,1)}), bf16[16,192,320]{2,1,0:T(8,128)(2,1)}, u32[]{:S(2)}, u32[]{:S(2)}) async-start(bf16[16,192,320]{2,1,0:T(8,128)(2,1)} %copy.85), calls=%async_computation | async-start | bytes 4718592 | tf_op jit(solution)/shard_map/all_to_all | solution.py:133
  21.4 9.3 %copy-start.12 = (bf16[8,2,4,512]{3,2,1,0:T(4,128)(2,1)S(1)}, bf16[8,2,4,512]{3,2,1,0:T(4,128)(2,1)}, u32[]{:S(2)}) copy-start(bf16[8,2,4,512]{3,2,1,0:T(4,128)(2,1)} %param.16) | copy-start | bytes 196612
  21.4 107.5 %copy-start.15 = (f32[512]{0:T(512)S(1)}, f32[512]{0:T(512)}, u32[]{:S(2)}) copy-start(f32[512]{0:T(512)} %param.18) | copy-start | bytes 6148
  21.4 107.5 %copy-start.16 = (f32[512]{0:T(512)S(1)}, f32[512]{0:T(512)}, u32[]{:S(2)}) copy-start(f32[512]{0:T(512)} %param.17) | copy-start | bytes 6148
  21.4 180.4 %copy-start.18 = (f32[16]{0:T(128)S(1)}, f32[16]{0:T(128)}, u32[]{:S(2)}) copy-start(f32[16]{0:T(128)} %param.20) | copy-start | bytes 196
  21.4 245.5 %all-gather.5.cloned.1.call-start = ((), (), s32[]{:S(2)}) async-start(), calls=%async_computation.2 | async-start | bytes 3342336 | tf_op jit(solution)/shard_map/all_gather | solution.py:143
  30.6 172.4 %copy-start.7 = (bf16[64,3072]{1,0:T(8,128)(2,1)S(1)}, bf16[64,3072]{1,0:T(8,128)(2,1)}, u32[]{:S(2)}) copy-start(bf16[64,3072]{1,0:T(8,128)(2,1)} %param.21) | copy-start | bytes 1179652
  30.6 172.4 %copy-start.11 = (f32[3072]{0:T(1024)S(1)}, f32[3072]{0:T(1024)}, u32[]{:S(2)}) copy-start(f32[3072]{0:T(1024)} %param.22) | copy-start | bytes 36868
  203.0 3.7 %copy-start.10 = (bf16[512,64]{1,0:T(8,128)(2,1)}, bf16[512,64]{1,0:T(8,128)(2,1)S(1)}, u32[]{:S(2)}) copy-start(bf16[512,64]{1,0:T(8,128)(2,1)S(1)} %reshape.100) | copy-start | bytes 196612
  203.0 3.6 %copy-start.17 = (f32[2,192]{1,0:T(2,128)S(1)}, f32[2,192]{1,0:T(2,128)}, u32[]{:S(2)}) copy-start(f32[2,192]{1,0:T(2,128)} %param.28) | copy-start | bytes 4612
  231.8 4.7 %copy-start.13 = (f32[3,3072]{1,0:T(4,128)S(1)}, f32[3,3072]{1,0:T(4,128)}, u32[]{:S(2)}) copy-start(f32[3,3072]{1,0:T(4,128)} %param.23) | copy-start | bytes 110596
  231.8 14.2 %collective-permute-start = (bf16[3072,5,64]{0,2,1:T(8,128)(2,1)}, bf16[3072,5,64]{0,2,1:T(8,128)(2,1)}, u32[]{:S(2)}, u32[]{:S(2)}) collective-permute-start(bf16[3072,5,64]{0,2,1:T(8,128)(2,1)} %reshape.103), channel_id=1, source_target_pairs={{0,2},{2,0},{4,6},{6,4},{8,10},{10,8},{12,14},{14,12},{16,18},{18,... | collective-permute-start | bytes 5898248 | tf_op jit(solution)/shard_map/ppermute | solution.py:17
  236.6 6.3 %copy-start.5 = (bf16[3072,5,64]{0,2,1:T(8,128)(2,1)S(1)}, bf16[3072,5,64]{0,2,1:T(8,128)(2,1)}, u32[]{:S(2)}) copy-start(bf16[3072,5,64]{0,2,1:T(8,128)(2,1)} %reshape.103) | copy-start | bytes 5898244
  254.3 3.5 %copy-start.3 = (bf16[3072,5,64]{2,0,1:T(8,128)(2,1)}, bf16[3072,5,64]{2,0,1:T(8,128)(2,1)S(1)}, u32[]{:S(2)}) copy-start(bf16[3072,5,64]{2,0,1:T(8,128)(2,1)S(1)} %get-tuple-element.12) | copy-start | bytes 5898244
  262.0 3.6 %copy-start.4 = (bf16[512,3072]{1,0:T(8,128)(2,1)S(1)}, bf16[512,3072]{1,0:T(8,128)(2,1)}, u32[]{:S(2)}) copy-start(bf16[512,3072]{1,0:T(8,128)(2,1)} %add_convert_fusion) | copy-start | bytes 9437188
  262.0 3.8 %copy-start.9 = (bf16[3072,2,128]{0,2,1:T(8,128)(2,1)S(1)}, bf16[3072,2,128]{0,2,1:T(8,128)(2,1)}, u32[]{:S(2)}) copy-start(bf16[3072,2,128]{0,2,1:T(8,128)(2,1)} %copy.91) | copy-start | bytes 4718596
  265.8 3.9 %copy-start.8 = (bf16[3072,2,128]{0,2,1:T(8,128)(2,1)S(1)}, bf16[3072,2,128]{0,2,1:T(8,128)(2,1)}, u32[]{:S(2)}) copy-start(bf16[3072,2,128]{0,2,1:T(8,128)(2,1)} %copy.93) | copy-start | bytes 4718596
  269.7 4.0 %copy-start.6 = (bf16[3072,512]{1,0:T(8,128)(2,1)S(1)}, bf16[3072,512]{1,0:T(8,128)(2,1)}, u32[]{:S(2)}) copy-start(bf16[3072,512]{1,0:T(8,128)(2,1)} %all-gather.5.cloned.1.call-done) | copy-start | bytes 9437188
  277.5 20.7 %copy-start.14 = (f32[3072]{0:T(1024)S(1)}, f32[3072]{0:T(1024)}, u32[]{:S(2)}) copy-start(f32[3072]{0:T(1024)} %param.31) | copy-start | bytes 36868
  277.5 10.5 %all-to-all-start.1 = ((bf16[16,16,128]{2,1,0:T(8,128)(2,1)}), bf16[16,16,128]{2,1,0:T(8,128)(2,1)S(1)}, u32[]{:S(2)}, u32[]{:S(2)}) async-start(bf16[16,16,128]{2,1,0:T(8,128)(2,1)} %bitcast.25), calls=%async_computation.1 | async-start | bytes 131072 | tf_op jit(solution)/shard_map/all_to_all | solution.py:198
  288.0 14.6 %copy-start.1 = (bf16[3,3,3,16,512]{4,3,2,1,0:T(8,128)(2,1)S(1)}, bf16[3,3,3,16,512]{4,3,2,1,0:T(8,128)(2,1)}, u32[]{:S(2)}) copy-start(bf16[3,3,3,16,512]{4,3,2,1,0:T(8,128)(2,1)} %param.19) | copy-start | bytes 1327108
  291.8 6.4 %collective-permute-start.1 = (f32[16,3072]{1,0:T(8,128)S(1)}, f32[16,3072]{1,0:T(8,128)S(1)}, u32[]{:S(2)}, u32[]{:S(2)}) collective-permute-start(f32[16,3072]{1,0:T(8,128)S(1)} %fusion.51), channel_id=1, source_target_pairs={{0,1},{1,0},{2,3},{3,2},{4,5},{5,4},{6,7},{7,6},{8,9},{9,8},{10,11... | collective-permute-start | bytes 589832 | tf_op jit(solution)/shard_map/ppermute | solution.py:213
  (1 other events, 3.4 us)
Sparse Core Ops, SparseCore 0:
  30.8 65.8 all-gather.4
